TPU v7x, 32 devices: a whole 2x2x4 slice. The times are simulated.
32 devices in a mesh: tm: 8 (over z, y), port: 4 (over x, core).
Axes of the slice: x: 2, y: 2, z: 4, core: 2. Of those that a mesh axis runs over, the one named last changes fastest.
Arguments:
- voltages: float32 [256, 131072], P('port', 'tm'), may hold values from -6 to 6
- currents: float32 [256, 131072], P('port', 'tm'), may hold values from -0.12 to 0.12
- impedance: float32 [256], P('port'), may hold values from 25 to 100
- freq_index: int32 [2048], replicated, may hold values from 1 to 65535
- window_start: int32 [256], P('port'), may hold values from 0 to 65535
- pairing: int32 [256], P('port'), may hold values from 0 to 255
Outputs:
- scattering: float32 [2, 256, 2048], P(None, 'port', 'tm')
All inputs are finite; a program needn't handle non-finite values.
Results may differ from a plain program's by a relative error of at most 0.011.
Values sent between devices are 32-bit elements; how exact they have to be, the bound alone decides.
A program may use at most 128 MiB of HBM per device.

v0:
```python
import math

import jax
import jax.numpy as jnp
from jax import lax
from jax.sharding import PartitionSpec as P


def angles(freq_index, times, total):
    high = freq_index // 512
    low = freq_index % 512
    stride = times * 512 % total
    phase = (stride[:, None] * high[None, :] % total + times[:, None] * low[None, :]) % total
    angle = phase.astype(jnp.float32) * (2.0 * math.pi / total)
    return (jnp.cos(angle), jnp.sin(angle))


def waves(v_re, v_im, c_re, c_im, impedance):
    zcol = impedance[:, None]
    root = 2.0 * jnp.sqrt(zcol)
    a_re = (v_re + zcol * c_re) / root
    a_im = (v_im + zcol * c_im) / root
    b_re = (v_re - zcol * c_re) / root
    b_im = (v_im - zcol * c_im) / root
    return (a_re, a_im, b_re, b_im)


def body(voltages, currents, impedance, freq_index, window_start, pairing):
    local_ports, local_times = voltages.shape
    width = freq_index.shape[0]
    tm_count = lax.axis_size("tm")
    total = local_times * tm_count
    first = lax.axis_index("tm") * local_times
    local = first + jnp.arange(local_times, dtype=jnp.int32)
    gate = local[None, :] >= window_start[:, None]
    gated_v = jnp.where(gate, voltages, 0.0).astype(jnp.bfloat16)
    gated_c = jnp.where(gate, currents, 0.0).astype(jnp.bfloat16)
    block = math.gcd(local_times, 4096)
    inner = min(block, 128)
    groups = block // inner
    base_cos, base_sin = angles(freq_index, jnp.arange(inner, dtype=jnp.int32), total)

    def accumulate(index, carry):
        start = index * block
        offsets = first + start + inner * jnp.arange(groups, dtype=jnp.int32)
        turn_cos, turn_sin = angles(freq_index, offsets, total)
        cos_part = (
            turn_cos[:, None, :] * base_cos[None] - turn_sin[:, None, :] * base_sin[None]
        ).astype(jnp.bfloat16)
        sin_part = (
            -(turn_sin[:, None, :] * base_cos[None] + turn_cos[:, None, :] * base_sin[None])
        ).astype(jnp.bfloat16)
        table = jnp.concatenate([cos_part, sin_part], axis=2).reshape(block, 2 * width)
        part_v = lax.dynamic_slice_in_dim(gated_v, start, block, 1)
        part_c = lax.dynamic_slice_in_dim(gated_c, start, block, 1)
        return (
            carry[0] + jnp.dot(part_v, table, preferred_element_type=jnp.float32),
            carry[1] + jnp.dot(part_c, table, preferred_element_type=jnp.float32),
        )

    empty = jnp.zeros((local_ports, 2 * width), jnp.float32)
    sum_v, sum_c = lax.fori_loop(0, local_times // block, accumulate, (empty, empty))
    scale = 1.0 / math.sqrt(total)
    lines = width // tm_count
    whole_v, whole_c = lax.psum((sum_v, sum_c), "tm")
    whole_v = whole_v * scale
    whole_c = whole_c * scale
    a_re, a_im, b_re, b_im = waves(
        whole_v[:, :width], whole_v[:, width:], whole_c[:, :width], whole_c[:, width:], impedance
    )
    power = a_re * a_re + a_im * a_im
    mean_power = jnp.sum(power, axis=1) / width + 1e-06
    offset = lax.axis_index("tm") * lines
    a_re = lax.dynamic_slice_in_dim(a_re, offset, lines, 1)
    a_im = lax.dynamic_slice_in_dim(a_im, offset, lines, 1)
    b_re = lax.dynamic_slice_in_dim(b_re, offset, lines, 1)
    b_im = lax.dynamic_slice_in_dim(b_im, offset, lines, 1)
    power = lax.dynamic_slice_in_dim(power, offset, lines, 1)
    every_re, every_im, every_mean = (
        lax.all_gather(a_re, "port", axis=0, tiled=True),
        lax.all_gather(a_im, "port", axis=0, tiled=True),
        lax.all_gather(mean_power, "port", axis=0, tiled=True),
    )
    q_re = jnp.take(every_re, pairing, axis=0)
    q_im = jnp.take(every_im, pairing, axis=0)
    q_mean = jnp.take(every_mean, pairing, axis=0)
    q_power = q_re * q_re + q_im * q_im
    denom = jnp.maximum(q_power, 0.1 * q_mean[:, None])
    s_re = (b_re * q_re + b_im * q_im) / denom
    s_im = (b_im * q_re - b_re * q_im) / denom
    return jnp.stack([s_re, s_im], axis=0)


def solution(mesh):
    placed = (P("port", "tm"), P("port", "tm"), P("port"), P(), P("port"), P("port"))
    return jax.shard_map(
        body, mesh=mesh, in_specs=placed, out_specs=P(None, "port", "tm"), check_vma=False
    )
```

profile of v0, /device:TPU:0, one launch (start us, length us, event | category | flops | bytes accessed | tf_op | source)
XLA Modules:
  0.0 348.2 jit_solution(2114511428757461816)
XLA Ops:
  6.5 0.0 all-reduce.4.cloned.1.call-start
  6.6 0.7 add_select_fusion.6
  7.3 5.6 %fusion.32 = (bf16[64,16384]{1,0:T(8,128)(2,1)S(1)}, bf16[64,16384]{1,0:T(8,128)(2,1)}) fusion(f32[64,16384]{1,0:T(8,128)} %param.11, s32[16384]{0:T(1024)S(1)} %iota_add_fusion, s32[64]{0:T(128)} %param.14, f32[64,16384]{1,0:T(8,128)} %param.10), kind=kLoop, calls=%fused_computation.65 | loop fusion | flops 3145728 | bytes 12648704 | tf_op jit(solution)/shard_map/convert_element_type | solution.py:37
  12.9 0.0 copy-start.3
  12.9 0.0 copy-start.2
  12.9 0.0 copy-start.1
  12.9 198.3 %while.22 = (s32[]{:T(128)}, f32[64,4096]{1,0:T(8,128)S(1)}, f32[64,4096]{1,0:T(8,128)}, bf16[64,16384]{1,0:T(8,128)(2,1)}, s32[]{:T(128)}, /*index=5*/s32[1,204...) while((s32[]{:T(128)}, f32[64,4096]{1,0:T(8,128)S(1)}, ...), condition=%wide.region_1.2_spmd.clone.clone.clone, body=%wide.region_0.1_spmd.clone.clone.clone.sunk | while | flops 4514624000 | bytes 111236320 | solution.py:62
  13.0 0.7 add_select_fusion.9
  13.7 1.2 fusion.46
  14.9 4.6 %fusion.45 = (f32[128,2048]{1,0:T(8,128)S(1)}, f32[128,2048]{1,0:T(8,128)S(1)}) fusion(s32[2048]{0:T(1024)S(1)} %get-tuple-element.664, s32[2048]{0:T(1024)S(1)} %get-tuple-element.662, s32[128]{0:T(128)S(1)} %get-tuple-element.663), kind=kLoop, calls=%fused_computation.26.clone.1 | loop fusion | flops 7077888 | bytes 2114048 | tf_op jit(solution)/shard_map/cos | solution.py:15
  19.5 15.4 %subtract_convert_fusion.2 = (bf16[32,128,2048]{2,1,0:T(8,128)(2,1)}, bf16[32,128,2048]{2,1,0:T(8,128)(2,1)}) fusion(f32[128,2048]{1,0:T(8,128)S(1)} %get-tuple-element.608, f32[32,2048]{1,0:T(8,128)S(1)} %get-tuple-element.613, f32[128,2048]{1,0:T(8,128)S(1)} %get-tuple-element.614, f32[32,2048]{1,0:T(8,128)S(1)} %get-tuple-element.615), kind=kLoop, calls=%fused_computation.7.clone.1 | loop fusion | flops 75497472 | bytes 36175872 | tf_op jit(solution)/shard_map/while/body/eval_jaxpr/convert_element_type | solution.py:49
  34.9 13.7 %fusion.48 = f32[64,4096]{1,0:T(8,128)} fusion(bf16[4096,2048]{1,0:T(8,128)(2,1)} %bitcast.18, bf16[4096,2048]{1,0:T(8,128)(2,1)} %bitcast.16, f32[64,4096]{1,0:T(8,128)} %get-tuple-element.637, bf16[64,16384]{1,0:T(8,128)(2,1)S(1)} %get-tuple-element.661, s32[]{:T(128)S(6)} %select_n.551, pred[]{:T(512)S(6)} %compare.43), kind=kOutput, calls=%fused_computation.11.clone.1 | convolution fusion | flops 2215116800 | bytes 36175876 | tf_op jit(solution)/shard_map/while/body/eval_jaxpr/dot_general | solution.py:58
  48.6 13.6 %fusion.47 = f32[64,4096]{1,0:T(8,128)S(1)} fusion(bf16[4096,2048]{1,0:T(8,128)(2,1)} %bitcast.19, bf16[4096,2048]{1,0:T(8,128)(2,1)} %bitcast.17, f32[64,4096]{1,0:T(8,128)S(1)} %get-tuple-element.636, bf16[64,16384]{1,0:T(8,128)(2,1)} %get-tuple-element.655, s32[]{:T(128)S(6)} %select_n.551, pred[]{:T(512)S(6)} %compare.43), kind=kOutput, calls=%fused_computation.10.clone.1 | convolution fusion | flops 2215116800 | bytes 36175876 | tf_op jit(solution)/shard_map/while/body/eval_jaxpr/dot_general | solution.py:57
  62.3 0.7 add_select_fusion.9
  63.0 1.2 fusion.46
  64.3 4.6 %fusion.45 = (f32[128,2048]{1,0:T(8,128)S(1)}, f32[128,2048]{1,0:T(8,128)S(1)}) fusion(s32[2048]{0:T(1024)S(1)} %get-tuple-element.664, s32[2048]{0:T(1024)S(1)} %get-tuple-element.662, s32[128]{0:T(128)S(1)} %get-tuple-element.663), kind=kLoop, calls=%fused_computation.26.clone.1 | loop fusion | flops 7077888 | bytes 2114048 | tf_op jit(solution)/shard_map/cos | solution.py:15
  68.9 15.4 %subtract_convert_fusion.2 = (bf16[32,128,2048]{2,1,0:T(8,128)(2,1)}, bf16[32,128,2048]{2,1,0:T(8,128)(2,1)}) fusion(f32[128,2048]{1,0:T(8,128)S(1)} %get-tuple-element.608, f32[32,2048]{1,0:T(8,128)S(1)} %get-tuple-element.613, f32[128,2048]{1,0:T(8,128)S(1)} %get-tuple-element.614, f32[32,2048]{1,0:T(8,128)S(1)} %get-tuple-element.615), kind=kLoop, calls=%fused_computation.7.clone.1 | loop fusion | flops 75497472 | bytes 36175872 | tf_op jit(solution)/shard_map/while/body/eval_jaxpr/convert_element_type | solution.py:49
  84.3 14.0 %fusion.48 = f32[64,4096]{1,0:T(8,128)} fusion(bf16[4096,2048]{1,0:T(8,128)(2,1)} %bitcast.18, bf16[4096,2048]{1,0:T(8,128)(2,1)} %bitcast.16, f32[64,4096]{1,0:T(8,128)} %get-tuple-element.637, bf16[64,16384]{1,0:T(8,128)(2,1)S(1)} %get-tuple-element.661, s32[]{:T(128)S(6)} %select_n.551, pred[]{:T(512)S(6)} %compare.43), kind=kOutput, calls=%fused_computation.11.clone.1 | convolution fusion | flops 2215116800 | bytes 36175876 | tf_op jit(solution)/shard_map/while/body/eval_jaxpr/dot_general | solution.py:58
  98.3 13.6 %fusion.47 = f32[64,4096]{1,0:T(8,128)S(1)} fusion(bf16[4096,2048]{1,0:T(8,128)(2,1)} %bitcast.19, bf16[4096,2048]{1,0:T(8,128)(2,1)} %bitcast.17, f32[64,4096]{1,0:T(8,128)S(1)} %get-tuple-element.636, bf16[64,16384]{1,0:T(8,128)(2,1)} %get-tuple-element.655, s32[]{:T(128)S(6)} %select_n.551, pred[]{:T(512)S(6)} %compare.43), kind=kOutput, calls=%fused_computation.10.clone.1 | convolution fusion | flops 2215116800 | bytes 36175876 | tf_op jit(solution)/shard_map/while/body/eval_jaxpr/dot_general | solution.py:57
  112.0 0.7 add_select_fusion.9
  112.7 1.2 fusion.46
  113.9 4.6 %fusion.45 = (f32[128,2048]{1,0:T(8,128)S(1)}, f32[128,2048]{1,0:T(8,128)S(1)}) fusion(s32[2048]{0:T(1024)S(1)} %get-tuple-element.664, s32[2048]{0:T(1024)S(1)} %get-tuple-element.662, s32[128]{0:T(128)S(1)} %get-tuple-element.663), kind=kLoop, calls=%fused_computation.26.clone.1 | loop fusion | flops 7077888 | bytes 2114048 | tf_op jit(solution)/shard_map/cos | solution.py:15
  118.5 15.4 %subtract_convert_fusion.2 = (bf16[32,128,2048]{2,1,0:T(8,128)(2,1)}, bf16[32,128,2048]{2,1,0:T(8,128)(2,1)}) fusion(f32[128,2048]{1,0:T(8,128)S(1)} %get-tuple-element.608, f32[32,2048]{1,0:T(8,128)S(1)} %get-tuple-element.613, f32[128,2048]{1,0:T(8,128)S(1)} %get-tuple-element.614, f32[32,2048]{1,0:T(8,128)S(1)} %get-tuple-element.615), kind=kLoop, calls=%fused_computation.7.clone.1 | loop fusion | flops 75497472 | bytes 36175872 | tf_op jit(solution)/shard_map/while/body/eval_jaxpr/convert_element_type | solution.py:49
  133.9 14.0 %fusion.48 = f32[64,4096]{1,0:T(8,128)} fusion(bf16[4096,2048]{1,0:T(8,128)(2,1)} %bitcast.18, bf16[4096,2048]{1,0:T(8,128)(2,1)} %bitcast.16, f32[64,4096]{1,0:T(8,128)} %get-tuple-element.637, bf16[64,16384]{1,0:T(8,128)(2,1)S(1)} %get-tuple-element.661, s32[]{:T(128)S(6)} %select_n.551, pred[]{:T(512)S(6)} %compare.43), kind=kOutput, calls=%fused_computation.11.clone.1 | convolution fusion | flops 2215116800 | bytes 36175876 | tf_op jit(solution)/shard_map/while/body/eval_jaxpr/dot_general | solution.py:58
  148.0 13.6 %fusion.47 = f32[64,4096]{1,0:T(8,128)S(1)} fusion(bf16[4096,2048]{1,0:T(8,128)(2,1)} %bitcast.19, bf16[4096,2048]{1,0:T(8,128)(2,1)} %bitcast.17, f32[64,4096]{1,0:T(8,128)S(1)} %get-tuple-element.636, bf16[64,16384]{1,0:T(8,128)(2,1)} %get-tuple-element.655, s32[]{:T(128)S(6)} %select_n.551, pred[]{:T(512)S(6)} %compare.43), kind=kOutput, calls=%fused_computation.10.clone.1 | convolution fusion | flops 2215116800 | bytes 36175876 | tf_op jit(solution)/shard_map/while/body/eval_jaxpr/dot_general | solution.py:57
  161.7 0.7 add_select_fusion.9
  162.4 1.2 fusion.46
  163.6 4.6 %fusion.45 = (f32[128,2048]{1,0:T(8,128)S(1)}, f32[128,2048]{1,0:T(8,128)S(1)}) fusion(s32[2048]{0:T(1024)S(1)} %get-tuple-element.664, s32[2048]{0:T(1024)S(1)} %get-tuple-element.662, s32[128]{0:T(128)S(1)} %get-tuple-element.663), kind=kLoop, calls=%fused_computation.26.clone.1 | loop fusion | flops 7077888 | bytes 2114048 | tf_op jit(solution)/shard_map/cos | solution.py:15
  168.2 15.4 %subtract_convert_fusion.2 = (bf16[32,128,2048]{2,1,0:T(8,128)(2,1)}, bf16[32,128,2048]{2,1,0:T(8,128)(2,1)}) fusion(f32[128,2048]{1,0:T(8,128)S(1)} %get-tuple-element.608, f32[32,2048]{1,0:T(8,128)S(1)} %get-tuple-element.613, f32[128,2048]{1,0:T(8,128)S(1)} %get-tuple-element.614, f32[32,2048]{1,0:T(8,128)S(1)} %get-tuple-element.615), kind=kLoop, calls=%fused_computation.7.clone.1 | loop fusion | flops 75497472 | bytes 36175872 | tf_op jit(solution)/shard_map/while/body/eval_jaxpr/convert_element_type | solution.py:49
  183.6 14.0 %fusion.48 = f32[64,4096]{1,0:T(8,128)} fusion(bf16[4096,2048]{1,0:T(8,128)(2,1)} %bitcast.18, bf16[4096,2048]{1,0:T(8,128)(2,1)} %bitcast.16, f32[64,4096]{1,0:T(8,128)} %get-tuple-element.637, bf16[64,16384]{1,0:T(8,128)(2,1)S(1)} %get-tuple-element.661, s32[]{:T(128)S(6)} %select_n.551, pred[]{:T(512)S(6)} %compare.43), kind=kOutput, calls=%fused_computation.11.clone.1 | convolution fusion | flops 2215116800 | bytes 36175876 | tf_op jit(solution)/shard_map/while/body/eval_jaxpr/dot_general | solution.py:58
  197.6 13.6 %fusion.47 = f32[64,4096]{1,0:T(8,128)S(1)} fusion(bf16[4096,2048]{1,0:T(8,128)(2,1)} %bitcast.19, bf16[4096,2048]{1,0:T(8,128)(2,1)} %bitcast.17, f32[64,4096]{1,0:T(8,128)S(1)} %get-tuple-element.636, bf16[64,16384]{1,0:T(8,128)(2,1)} %get-tuple-element.655, s32[]{:T(128)S(6)} %select_n.551, pred[]{:T(512)S(6)} %compare.43), kind=kOutput, calls=%fused_computation.10.clone.1 | convolution fusion | flops 2215116800 | bytes 36175876 | tf_op jit(solution)/shard_map/while/body/eval_jaxpr/dot_general | solution.py:57
  211.3 0.0 copy-start
  211.3 1.0 copy-done
  212.2 0.0 all-reduce.4.cloned.1.call-update
  212.3 0.0 copy-done.3
  212.3 0.6 dynamic-slice
  213.5 0.0 copy-done.2
  213.6 0.0 copy-done.1
  213.6 103.9 %all-reduce.4.cloned.1.call-done = (f32[64,4096]{1,0:T(8,128)}, f32[64,4096]{1,0:T(8,128)}) async-done(((f32[64,4096]{1,0:T(8,128)}, f32[64,4096]{1,0:T(8,128)}), (f32[64,4096]{1,0:T(8,128)}, f32[64,4096]{1,0:T(8,128)})) %all-reduce.4.cloned.1.call-update) | async-done | bytes 2097168 | tf_op jit(solution)/shard_map/psum | solution.py:65
  317.5 1.7 broadcast_multiply_fusion
  319.2 0.4 add_reduce_fusion
  319.7 5.8 %all_gather.9 = f32[256,256]{1,0:T(8,128)S(1)} all-gather(f32[64,256]{1,0:T(8,128)S(1)} %constant_dynamic-slice_fusion.1), channel_id=1, replica_groups=mesh['tm'=8,'port'=4] {'port'}, dimensions={0}, use_global_device_ids=true | all-gather | bytes 327680 | tf_op jit(solution)/shard_map/all_gather | solution.py:80
  325.4 5.8 %all_gather.10 = f32[256,256]{1,0:T(8,128)S(1)} all-gather(f32[64,256]{1,0:T(8,128)S(1)} %constant_dynamic-slice_fusion), channel_id=1, replica_groups=mesh['tm'=8,'port'=4] {'port'}, dimensions={0}, use_global_device_ids=true | all-gather | bytes 327680 | tf_op jit(solution)/shard_map/all_gather | solution.py:81
  331.3 0.7 gather_fusion.1
  331.9 0.7 gather_fusion.2
  332.6 0.1 add_dynamic-update-slice_fusion
  332.7 7.0 %all-reduce = f32[256]{0:T(256)S(1)} all-reduce(f32[256]{0:T(256)S(1)} %add_dynamic-update-slice_fusion), channel_id=1, replica_groups=mesh['tm'=8,'port'=4] {'port'}, use_global_device_ids=true, to_apply=%add | all-reduce | flops 256 | bytes 2048
  339.7 0.8 gather_fusion
  340.5 0.1 divide_bitcast_fusion.1
  340.7 0.7 pad_maximum_fusion.7
  (19 shorter events, 0.3 us)
Async XLA Ops:
  6.5 310.9 %all-reduce.4.cloned.1.call-start = ((), (), s32[]{:S(2)}) async-start(), calls=%async_computation | async-start | bytes 4194304 | tf_op jit(solution)/shard_map/psum | solution.py:65
  12.9 199.4 %copy-start.3 = (u32[32]{0:T(128)S(1)}, u32[32]{0:T(128)}, u32[]{:S(2)}) copy-start(u32[32]{0:T(128)} %constant.290) | copy-start | bytes 388
  12.9 200.6 %copy-start.2 = (s32[64]{0:T(128)S(1)}, s32[64]{0:T(128)}, u32[]{:S(2)}) copy-start(s32[64]{0:T(128)} %param.15) | copy-start | bytes 772
  12.9 200.6 %copy-start.1 = (f32[64]{0:T(128)S(1)}, f32[64]{0:T(128)}, u32[]{:S(2)}) copy-start(f32[64]{0:T(128)} %param.12) | copy-start | bytes 772
  211.3 1.0 copy-start
Sparse Core Ops, SparseCore 0:
  212.4 105.0 all-reduce.3
where the time goes:
time: 349 us; the launch traced here: 348 us
  matrix products  110 us (32%)
  waiting for transfers between devices  104 us (30%)
  other arithmetic  97.4 us (28%)
  blocking collectives  18.7 us (5%)
  between operations  14.2 us (4%)
  local copies, waits for them, and re-layouts  3.68 us (1%)
    psum x1, waiting for transfers between devices, body(): whole_v, whole_c = lax.psum((sum_v, sum_c), 'tm')  104 us
    convert_element_type x4, other arithmetic, accumulate(): cos_part = (turn_cos[:, None, :] * base_cos[None] - turn_sin[:, None, :]...  61.7 us
    dot_general x4, matrix products, accumulate(): jnp.dot(part_c, table, preferred_element_type=jnp.float32)  55.8 us
    dot_general x4, matrix products, accumulate(): jnp.dot(part_v, table, preferred_element_type=jnp.float32)  54.5 us
    cos x8, other arithmetic, angles(): return (jnp.cos(angle), jnp.sin(angle))  23.2 us
    unnamed x1, blocking collectives  7.04 us
  transfers between devices with their start and end apart: 1, of which 1 were waited for; matrix products, arithmetic and copies ran while one was open for 0% of the time, Pallas kernels for 0%

commit v1 on v0

v1 whole, which is shorter than its diff:
```python
import functools
import math

import jax
import jax.numpy as jnp
from jax import lax
from jax.experimental import pallas as pl
from jax.experimental.pallas import tpu as pltpu
from jax.sharding import PartitionSpec as P

BASE = 32
F32 = jnp.float32


def kernel(
    sizes,
    v_hbm, c_hbm, cos_ref, sin_ref, z_ref, start_ref, pair_ref,
    out_ref,
    xv, xc, xe, xo, tab_c, tab_s, away, own, y_recv, z_recv, gath, pbuf, mbuf, mcol, qa, qm,
    load_sem, y_send, y_got, z_send, z_got, g_send, g_got, p_send, p_got, m_send, m_got,
):
    n_tm, n_in, n_port, ports, half, blocks, lines, groups, width = sizes
    n_out = n_tm // n_in
    rows = 2 * ports
    me = lax.axis_index("tm")
    port = lax.axis_index("port")
    outer, inner = me // n_in, lax.rem(me, n_in)
    span = 2 * half

    def load(block, which):
        source, target = ((v_hbm, xv), (c_hbm, xc))[which]
        return pltpu.make_async_copy(
            source.at[:, pl.ds(pl.multiple_of(block * span, span), span)],
            target.at[:, pl.ds(pl.multiple_of(block * span, span), span)],
            load_sem.at[which, block],
        )

    for block in range(blocks):
        for which in range(2):
            load(block, which).start()

    barrier = pltpu.get_barrier_semaphore()
    for step in range(1, n_tm):
        pl.semaphore_signal(barrier, inc=1, device_id={"tm": lax.rem(me + step, n_tm)})
    for step in range(1, n_port):
        pl.semaphore_signal(barrier, inc=1, device_id={"port": lax.rem(port + step, n_port)})

    flip = (
        lax.broadcasted_iota(jnp.int32, (128, 128), 0)
        + lax.broadcasted_iota(jnp.int32, (128, 128), 1)
        == 127
    ).astype(F32).astype(jnp.bfloat16)
    tiles = half // 128
    lane = lax.broadcasted_iota(jnp.int32, (ports, 128), 1)
    starts = jnp.broadcast_to(start_ref[...], (ports, 128)) - me * (blocks * span) - lane

    def fold(block, carry):
        for which in range(2):
            load(block, which).wait()
            ref = (xv, xc)[which]

            def piece(tile):
                at = pl.multiple_of(block * span + tile * 128, 128)
                entries = jnp.where(starts <= at, ref[:, pl.ds(at, 128)], 0.0)
                return entries.astype(jnp.bfloat16)

            at_row = pl.multiple_of(block * rows + which * ports, ports)
            for tile in range(tiles):
                later = piece(tiles + tile).astype(F32)
                earlier = jnp.dot(piece(tiles - 1 - tile), flip, preferred_element_type=F32)
                xe[pl.ds(at_row, ports), tile * 128:(tile + 1) * 128] = (later + earlier).astype(jnp.bfloat16)
                xo[pl.ds(at_row, ports), tile * 128:(tile + 1) * 128] = (later - earlier).astype(jnp.bfloat16)
        return carry

    lax.fori_loop(0, blocks, fold, 0)
    pl.semaphore_wait(barrier, n_tm - 1 + n_port - 1)

    def spectra(owner, store):
        at = pl.ds(pl.multiple_of(owner * lines, lines), lines)
        bc, bs = cos_ref[0:BASE, at], sin_ref[0:BASE, at]
        for g in range(groups):
            tc, ts = cos_ref[BASE + g:BASE + g + 1, at], sin_ref[BASE + g:BASE + g + 1, at]
            tab_c[g * BASE:(g + 1) * BASE, :] = (tc * bc - ts * bs).astype(jnp.bfloat16)
            tab_s[g * BASE:(g + 1) * BASE, :] = (ts * bc + tc * bs).astype(jnp.bfloat16)
        even = jnp.dot(xe[...], tab_c[...], preferred_element_type=F32)
        odd = jnp.dot(xo[...], tab_s[...], preferred_element_type=F32)
        re = jnp.zeros((rows, lines), F32)
        im = jnp.zeros((rows, lines), F32)
        for block in range(blocks):
            k = BASE + groups + block
            pc, ps = cos_ref[k:k + 1, at], sin_ref[k:k + 1, at]
            e, o = even[block * rows:(block + 1) * rows], odd[block * rows:(block + 1) * rows]
            re = re + (pc * e - ps * o)
            im = im - (ps * e + pc * o)
        store[:, 0:lines] = re
        store[:, lines:2 * lines] = im

    def y_copy(k, r):
        return pltpu.make_async_remote_copy(
            src_ref=away.at[k, r], dst_ref=y_recv.at[k, r],
            send_sem=y_send.at[k, r], recv_sem=y_got.at[k, r],
            device_id={"tm": outer * n_in + lax.rem(inner + 1 + r, n_in)},
        )

    def z_copy(k):
        return pltpu.make_async_remote_copy(
            src_ref=own.at[k], dst_ref=z_recv.at[k],
            send_sem=z_send.at[k], recv_sem=z_got.at[k],
            device_id={"tm": lax.rem(outer + k + 1, n_out) * n_in + inner},
        )

    def collect(k):
        for r in range(n_in - 1):
            y_copy(k, r).wait_recv()
            own[k] = own[k] + y_recv[k, r]

    def stage(k, carry):
        target = lax.rem(outer + k + 1, n_out)
        for r in range(n_in - 1):
            spectra(target * n_in + lax.rem(inner + 1 + r, n_in), away.at[k, r])
            y_copy(k, r).start()
        spectra(target * n_in + inner, own.at[k])

        @pl.when(k >= 1)
        def _():
            collect(k - 1)
            z_copy(k - 1).start()

        return carry

    lax.fori_loop(0, n_out, stage, 0)
    collect(n_out - 1)
    total = own[n_out - 1]
    for k in range(n_out - 1):
        z_copy(k).wait_recv()
        total = total + z_recv[k]

    volts, amps = total[0:ports], total[ports:rows]
    zcol = z_ref[...]
    root = 2.0 * jnp.sqrt(zcol)
    a = (volts + zcol * amps) / root
    b = (volts - zcol * amps) / root
    mine = pl.ds(pl.multiple_of(port * ports, ports), ports)
    gath[mine, :] = a

    def g_copy(step):
        return pltpu.make_async_remote_copy(
            src_ref=gath.at[mine, :], dst_ref=gath.at[mine, :],
            send_sem=g_send.at[step - 1], recv_sem=g_got.at[step - 1],
            device_id={"port": lax.rem(port + step, n_port)},
        )

    def p_copy(step):
        return pltpu.make_async_remote_copy(
            src_ref=pbuf.at[0], dst_ref=pbuf.at[step],
            send_sem=p_send.at[step - 1], recv_sem=p_got.at[step - 1],
            device_id={"tm": lax.rem(me + step, n_tm)},
        )

    def m_copy(step):
        return pltpu.make_async_remote_copy(
            src_ref=mbuf.at[port], dst_ref=mbuf.at[port],
            send_sem=m_send.at[step - 1], recv_sem=m_got.at[step - 1],
            device_id={"port": lax.rem(port + step, n_port)},
        )

    a_re, a_im = a[:, 0:lines], a[:, lines:2 * lines]
    power = jnp.sum(a_re * a_re + a_im * a_im, axis=1, keepdims=True)
    diagonal = lane == lax.broadcasted_iota(jnp.int32, (ports, 128), 0)
    packed = jnp.sum(jnp.where(diagonal, power, 0.0), axis=0, keepdims=True)
    pbuf[0] = jnp.broadcast_to(packed, (8, 128))
    for step in range(1, n_tm):
        p_copy(step).start()
    for step in range(1, n_port):
        g_copy(step).start()
    powers = pbuf[0]
    for step in range(1, n_tm):
        p_copy(step).wait_recv()
        powers = powers + pbuf[step]
    mbuf[port] = powers / width + 1e-06
    for step in range(1, n_port):
        m_copy(step).start()
    for step in range(1, n_port):
        m_copy(step).wait_recv()
    for index in range(n_port):
        spread = jnp.broadcast_to(mbuf[index][0:1, :], (ports, 128))
        column = jnp.sum(jnp.where(diagonal, spread, 0.0), axis=1, keepdims=True)
        mcol[index * ports:(index + 1) * ports, :] = jnp.broadcast_to(column, (ports, 128))
    for step in range(1, n_port):
        g_copy(step).wait_recv()
    for p in range(ports):
        q = pair_ref[p]
        qa[p:p + 1, :] = gath[pl.ds(q, 1), :]
        qm[p:p + 1, :] = mcol[pl.ds(q, 1), :]
    q_re, q_im = qa[:, 0:lines], qa[:, lines:2 * lines]
    denom = jnp.maximum(q_re * q_re + q_im * q_im, 0.1 * qm[:, 0:1])
    b_re, b_im = b[:, 0:lines], b[:, lines:2 * lines]
    out_ref[0] = (b_re * q_re + b_im * q_im) / denom
    out_ref[1] = (b_im * q_re - b_re * q_im) / denom

    for k in range(n_out):
        for r in range(n_in - 1):
            y_copy(k, r).wait_send()
    for k in range(n_out - 1):
        z_copy(k).wait_send()
    for step in range(1, n_tm):
        p_copy(step).wait_send()
    for step in range(1, n_port):
        g_copy(step).wait_send()
        m_copy(step).wait_send()


def body(n_tm, n_port, voltages, currents, impedance, freq_index, window_start, pairing):
    ports, local_times = voltages.shape
    width = freq_index.shape[0]
    total = local_times * n_tm
    assert total & (total - 1) == 0 and ports <= 128
    half = math.gcd(local_times // 2, 1024)
    blocks = local_times // (2 * half)
    groups = half // BASE
    lines = width // n_tm
    n_in = 2 if n_tm < 16 else 4
    n_out = n_tm // n_in
    rows = 2 * ports
    first = lax.axis_index("tm") * local_times
    odd_steps = 2 * jnp.arange(BASE, dtype=jnp.int32) + 1
    turns = 2 * BASE * jnp.arange(groups, dtype=jnp.int32)
    centres = 2 * first + 4 * half * jnp.arange(blocks, dtype=jnp.int32) + 2 * half - 1
    steps = jnp.concatenate([odd_steps, turns, centres])
    scale = jnp.where(jnp.arange(steps.shape[0]) < BASE + groups, 1.0, 1.0 / math.sqrt(total)).astype(F32)
    phase = (steps[:, None] * freq_index[None, :]) & (2 * total - 1)
    angle = phase.astype(F32) * (math.pi / total)
    cosines = jnp.cos(angle) * scale[:, None]
    sines = jnp.sin(angle) * scale[:, None]

    sizes = (n_tm, n_in, n_port, ports, half, blocks, lines, groups, width)
    vmem = pl.BlockSpec(memory_space=pltpu.VMEM)
    dma = pltpu.SemaphoreType.DMA
    return pl.pallas_call(
        functools.partial(kernel, sizes),
        out_shape=jax.ShapeDtypeStruct((2, ports, lines), F32),
        in_specs=[
            pl.BlockSpec(memory_space=pl.ANY), pl.BlockSpec(memory_space=pl.ANY),
            vmem, vmem, vmem, vmem, pl.BlockSpec(memory_space=pltpu.SMEM),
        ],
        out_specs=vmem,
        scratch_shapes=[
            pltpu.VMEM((ports, local_times), F32),
            pltpu.VMEM((ports, local_times), F32),
            pltpu.VMEM((blocks * rows, half), jnp.bfloat16),
            pltpu.VMEM((blocks * rows, half), jnp.bfloat16),
            pltpu.VMEM((half, lines), jnp.bfloat16),
            pltpu.VMEM((half, lines), jnp.bfloat16),
            pltpu.VMEM((n_out, n_in - 1, rows, 2 * lines), F32),
            pltpu.VMEM((n_out, rows, 2 * lines), F32),
            pltpu.VMEM((n_out, n_in - 1, rows, 2 * lines), F32),
            pltpu.VMEM((n_out - 1, rows, 2 * lines), F32),
            pltpu.VMEM((n_port * ports, 2 * lines), F32),
            pltpu.VMEM((n_tm, 8, 128), F32),
            pltpu.VMEM((n_port, 8, 128), F32),
            pltpu.VMEM((n_port * ports, 128), F32),
            pltpu.VMEM((ports, 2 * lines), F32),
            pltpu.VMEM((ports, 128), F32),
            dma((2, blocks)),
            dma((n_out, n_in - 1)), dma((n_out, n_in - 1)),
            dma((n_out - 1,)), dma((n_out - 1,)),
            dma((n_port - 1,)), dma((n_port - 1,)),
            dma((n_tm - 1,)), dma((n_tm - 1,)),
            dma((n_port - 1,)), dma((n_port - 1,)),
        ],
        compiler_params=pltpu.CompilerParams(
            collective_id=0, has_side_effects=True, vmem_limit_bytes=56 * 2**20
        ),
        name="spectra",
    )(voltages, currents, cosines, sines, impedance[:, None], window_start[:, None], pairing)


def solution(mesh):
    placed = (P("port", "tm"), P("port", "tm"), P("port"), P(), P("port"), P("port"))
    return jax.shard_map(
        functools.partial(body, mesh.shape["tm"], mesh.shape["port"]),
        mesh=mesh, in_specs=placed, out_specs=P(None, "port", "tm"), check_vma=False,
    )
```

time: 349 us -> 58.6 us (0.17)
  matrix products: 110 us -> 0 us
  waiting for transfers between devices: 104 us -> 0 us
  other arithmetic: 97.4 us -> 3.95 us
  Pallas kernels: 0 us -> 49.6 us
  blocking collectives: 18.7 us -> 0 us
  between operations: 14.2 us -> 0.01 us
    dot_general x8 -> x0, matrix products: 110 us -> none  [the longest x4 55.8 us: accumulate(): jnp.dot(part_c, table, preferred_element_type=jnp.float32)]
    psum x1 -> x0, waiting for transfers between devices: 104 us -> none  [body(): whole_v, whole_c = lax.psum((sum_v, sum_c), 'tm')]
    convert_element_type x5 -> x0, other arithmetic: 67.3 us -> none  [the longest x4 61.7 us: accumulate(): cos_part = (turn_cos[:, None, :] * base_cos[None] - turn_sin[:, None, :]...]
    pallas_call x0 -> x1, Pallas kernels: none -> 49.6 us  [body(): pl.pallas_call(functools.partial(kernel, sizes), out_shape=jax.ShapeDtype...]
    cos x8 -> x0, other arithmetic: 23.2 us -> none  [angles(): return (jnp.cos(angle), jnp.sin(angle))]
    all_gather x2 -> x0, blocking collectives: 11.6 us -> none  [the longest x1 5.84 us: body(): lax.all_gather(a_im, 'port', axis=0, tiled=True)]
    unnamed x1 -> x0, blocking collectives: 7.04 us -> none
    select_n x11 -> x1, other arithmetic: 3.61 us -> 0.01 us  [body(): jnp.where(jnp.arange(steps.shape[0]) < BASE + groups, 1.0, 1.0 / math.sqr...]
  transfers between devices with their start and end apart: 1 -> 0, of which waited for: 1 -> 0; matrix products, arithmetic and copies ran while one was open for 0% -> 0% of each run, Pallas kernels for 0% -> 0%
where the time goes in v1:
time: 58.6 us; the launch traced here: 57.8 us
  Pallas kernels  49.6 us (85%)
  local copies, waits for them, and re-layouts  4.27 us (7%)
  other arithmetic  3.95 us (7%)
    pallas_call x1, Pallas kernels, body(): pl.pallas_call(functools.partial(kernel, sizes), out_shape=jax.ShapeDtype...  49.6 us
    mul x1, other arithmetic, body(): sines = jnp.sin(angle) * scale[:, None]  3.86 us
    unnamed x1, local copies, waits for them, and re-layouts  1.57 us
    broadcast_in_dim x1, local copies, waits for them, and re-layouts, body(): impedance[:, None]  1.36 us
    broadcast_in_dim x1, local copies, waits for them, and re-layouts, body(): window_start[:, None]  1.34 us

profile of v1, /device:TPU:0, one launch (start us, length us, event | category | flops | bytes accessed | tf_op | source)
XLA Modules:
  0.0 57.8 jit_solution(4563292947906720439)
XLA Ops:
  0.0 0.1 pad_add_fusion
  0.1 1.4 %copy.7.z_ref = f32[64,1]{1,0:T(8,128)} copy(f32[64,1]{0,1:T(1,128)} %bitcast.2) | data formatting | bytes 512 | tf_op jit(solution)/shard_map/broadcast_in_dim | solution.py:275
  1.5 1.3 %copy.8.start_ref = s32[64,1]{1,0:T(8,128)} copy(s32[64,1]{0,1:T(1,128)} %bitcast.3) | data formatting | bytes 512 | tf_op jit(solution)/shard_map/broadcast_in_dim | solution.py:275
  2.8 3.9 %sine_multiply_fusion = (f32[72,2048]{1,0:T(8,128)}, f32[72,2048]{1,0:T(8,128)}) fusion(f32[72]{0:T(128)S(1)} %compare_select_fusion, s32[2048]{0:T(1024)} %param.9, s32[72]{0:T(128)S(1)} %pad_add_fusion), kind=kLoop, calls=%fused_computation | loop fusion | flops 884736 | bytes 1188416 | tf_op jit(solution)/shard_map/mul | solution.py:234
  6.7 49.6 %spectra.1 = f32[2,64,256]{2,1,0:T(8,128)} custom-call(f32[64,16384]{1,0:T(8,128)} %v_hbm.1, f32[64,16384]{1,0:T(8,128)} %c_hbm.1, f32[72,2048]{1,0:T(8,128)} %get-tuple-element.6.cos_ref, f32[72,2048]{1,0:T(8,128)} %get-tuple-element.5.sin_ref, f32[64,1]{1,0:T(8,128)} %copy.7.z_ref, s32[64,1]{1,0:T(8,128)} %copy.8.start_ref, s32[64]{0:T(128)} %pair_ref.1), custom_call_target="tpu_custom_call" | custom-call | tf_op jit(solution)/shard_map/spectra/pallas_call | solution.py:239
  56.2 1.6 %copy.10 = f32[2,64,256]{2,1,0:T(8,128)} copy(f32[2,64,256]{2,1,0:T(8,128)} %spectra.1) | data formatting | bytes 262144
  (3 shorter events, 0.0 us)

commit v2 on v1

v2 whole, which is shorter than its diff:
```python
import functools
import math

import jax
import jax.numpy as jnp
from jax import lax
from jax.experimental import pallas as pl
from jax.experimental.pallas import tpu as pltpu
from jax.sharding import PartitionSpec as P

BASE = 32
F32 = jnp.float32


def kernel(
    sizes,
    v_hbm, c_hbm, freq_ref, z_ref, start_ref, pair_ref,
    out_ref,
    cos_ref, sin_ref,
    xv, xc, xe, xo, tab_c, tab_s, away, own, y_recv, z_recv, gath, pbuf, mbuf, mcol, qa, qm,
    load_sem, y_send, y_got, z_send, z_got, g_send, g_got, p_send, p_got, m_send, m_got,
):
    n_tm, n_in, n_port, ports, half, blocks, lines, groups, width, subs = sizes
    sub = lines // subs
    n_out = n_tm // n_in
    rows = 2 * ports
    me = lax.axis_index("tm")
    port = lax.axis_index("port")
    outer, inner = me // n_in, lax.rem(me, n_in)
    span = 2 * half

    def load(block, which):
        source, target = ((v_hbm, xv), (c_hbm, xc))[which]
        return pltpu.make_async_copy(
            source.at[:, pl.ds(pl.multiple_of(block * span, span), span)],
            target.at[:, pl.ds(pl.multiple_of(block * span, span), span)],
            load_sem.at[which, block],
        )

    for block in range(blocks):
        for which in range(2):
            load(block, which).start()

    barrier = pltpu.get_barrier_semaphore()
    for step in range(1, n_tm):
        pl.semaphore_signal(barrier, inc=1, device_id={"tm": lax.rem(me + step, n_tm)})
    for step in range(1, n_port):
        pl.semaphore_signal(barrier, inc=1, device_id={"port": lax.rem(port + step, n_port)})

    flip = (
        lax.broadcasted_iota(jnp.int32, (128, 128), 0)
        + lax.broadcasted_iota(jnp.int32, (128, 128), 1)
        == 127
    ).astype(F32).astype(jnp.bfloat16)
    tiles = half // 128
    lane = lax.broadcasted_iota(jnp.int32, (ports, 128), 1)
    square = lax.broadcasted_iota(jnp.int32, (ports, ports), 0) == lax.broadcasted_iota(
        jnp.int32, (ports, ports), 1
    )

    def column_of(row):
        return jnp.sum(jnp.where(square, row, 0.0), axis=1, keepdims=True)

    zcol = column_of(z_ref[...])
    start_column = column_of(start_ref[...].astype(F32)).astype(jnp.int32)
    starts = jnp.broadcast_to(start_column, (ports, 128)) - me * (blocks * span) - lane

    whole = n_tm * blocks * span
    quarter_bits = (whole // 2).bit_length() - 1
    freq = freq_ref[...]
    count = lax.broadcasted_iota(jnp.int32, (8, 1), 0)
    for at in range(0, BASE + groups + blocks, 8):
        scale = 1.0
        if at < BASE:
            steps = 2 * (count + at) + 1
        elif at < BASE + groups:
            steps = 2 * BASE * (count + (at - BASE))
        else:
            scale = 1.0 / math.sqrt(whole)
            steps = me * (2 * blocks * span) + 4 * half * (count + (at - BASE - groups)) + (2 * half - 1)
        phase = (steps * freq) & (2 * whole - 1)
        quarter = (phase + whole // 4) >> quarter_bits
        x = (phase - (quarter << quarter_bits)).astype(F32) * (math.pi / whole)
        xx = x * x
        s = x * (1.0 + xx * (-1 / 6 + xx * (1 / 120 + xx * (-1 / 5040 + xx * (1 / 362880)))))
        c = 1.0 + xx * (-1 / 2 + xx * (1 / 24 + xx * (-1 / 720 + xx * (1 / 40320))))
        swap = (quarter & 1) == 1
        cosine, sine = jnp.where(swap, s, c), jnp.where(swap, c, s)
        cos_ref[at:at + 8, :] = jnp.where(((quarter + 1) & 2) == 2, -cosine, cosine) * scale
        sin_ref[at:at + 8, :] = jnp.where((quarter & 2) == 2, -sine, sine) * scale

    def fold(block, carry):
        for which in range(2):
            load(block, which).wait()
            ref = (xv, xc)[which]

            def piece(tile):
                at = pl.multiple_of(block * span + tile * 128, 128)
                entries = jnp.where(starts <= at, ref[:, pl.ds(at, 128)], 0.0)
                return entries.astype(jnp.bfloat16)

            at_row = pl.multiple_of(block * rows + which * ports, ports)
            for tile in range(tiles):
                later = piece(tiles + tile).astype(F32)
                earlier = jnp.dot(piece(tiles - 1 - tile), flip, preferred_element_type=F32)
                xe[pl.ds(at_row, ports), tile * 128:(tile + 1) * 128] = (later + earlier).astype(jnp.bfloat16)
                xo[pl.ds(at_row, ports), tile * 128:(tile + 1) * 128] = (later - earlier).astype(jnp.bfloat16)
        return carry

    lax.fori_loop(0, blocks, fold, 0)
    pl.semaphore_wait(barrier, n_tm - 1 + n_port - 1)

    def spectra(owner, store):
        at = pl.ds(pl.multiple_of(owner * lines, lines), lines)
        bc, bs = cos_ref[0:BASE, at], sin_ref[0:BASE, at]
        for g in range(groups):
            tc, ts = cos_ref[BASE + g:BASE + g + 1, at], sin_ref[BASE + g:BASE + g + 1, at]
            tab_c[g * BASE:(g + 1) * BASE, :] = (tc * bc - ts * bs).astype(jnp.bfloat16)
            tab_s[g * BASE:(g + 1) * BASE, :] = (ts * bc + tc * bs).astype(jnp.bfloat16)
        even = jnp.dot(xe[...], tab_c[...], preferred_element_type=F32)
        odd = jnp.dot(xo[...], tab_s[...], preferred_element_type=F32)
        re = jnp.zeros((rows, lines), F32)
        im = jnp.zeros((rows, lines), F32)
        for block in range(blocks):
            k = BASE + groups + block
            pc, ps = cos_ref[k:k + 1, at], sin_ref[k:k + 1, at]
            e, o = even[block * rows:(block + 1) * rows], odd[block * rows:(block + 1) * rows]
            re = re + (pc * e - ps * o)
            im = im - (ps * e + pc * o)
        for h in range(subs):
            store[h, :, 0:sub] = re[:, h * sub:(h + 1) * sub]
            store[h, :, sub:2 * sub] = im[:, h * sub:(h + 1) * sub]

    def destination(k):
        code, step, place, bit = 0, n_out - 1 - k, outer, 1
        for _ in range((n_out - 1).bit_length()):
            one, two = lax.rem(step, 2), lax.rem(place, 2)
            code = code + bit * (one + two - 2 * one * two)
            step, place, bit = step // 2, place // 2, 2 * bit
        return code

    def y_copy(k, r, h):
        return pltpu.make_async_remote_copy(
            src_ref=away.at[k, r, h], dst_ref=y_recv.at[k, r, h],
            send_sem=y_send.at[k, r, h], recv_sem=y_got.at[k, r, h],
            device_id={"tm": outer * n_in + lax.rem(inner + 1 + r, n_in)},
        )

    def z_copy(k, d, h, side):
        step = 1 - 2 * side
        return pltpu.make_async_remote_copy(
            src_ref=own.at[k, h], dst_ref=z_recv.at[side, d, h],
            send_sem=z_send.at[k, h], recv_sem=z_got.at[side, d, h],
            device_id={"tm": (outer + step) * n_in + inner},
        )

    def add_side(k, d, h, side):
        @pl.when(outer > 0 if side == 0 else outer < n_out - 1)
        def _():
            z_copy(k, d, h, side).wait_recv()
            own[k, h] = own[k, h] + z_recv[side, d, h]

    def collect(k, h):
        for r in range(n_in - 1):
            y_copy(k, r, h).wait_recv()
            own[k, h] = own[k, h] + y_recv[k, r, h]

    def service(k):
        d = destination(k)
        for h in range(subs):
            collect(k, h)

            @pl.when(d > outer)
            def _():
                add_side(k, d, h, 0)
                z_copy(k, d, h, 0).start()

            @pl.when(d < outer)
            def _():
                add_side(k, d, h, 1)
                z_copy(k, d, h, 1).start()

    def stage(k, carry):
        target = destination(k)
        for r in range(n_in - 1):
            spectra(target * n_in + lax.rem(inner + 1 + r, n_in), away.at[k, r])
            for h in range(subs):
                y_copy(k, r, h).start()
        spectra(target * n_in + inner, own.at[k])

        @pl.when(k >= 1)
        def _():
            service(k - 1)

        return carry

    lax.fori_loop(0, n_out, stage, 0)

    mine = pl.ds(pl.multiple_of(port * ports, ports), ports)

    def g_copy(step, h):
        return pltpu.make_async_remote_copy(
            src_ref=gath.at[h, mine, :], dst_ref=gath.at[h, mine, :],
            send_sem=g_send.at[step - 1, h], recv_sem=g_got.at[step - 1, h],
            device_id={"port": lax.rem(port + step, n_port)},
        )

    root = 2.0 * jnp.sqrt(zcol)
    power = jnp.zeros((ports, 1), F32)
    for h in range(subs):
        collect(n_out - 1, h)
        add_side(n_out - 1, outer, h, 0)
        add_side(n_out - 1, outer, h, 1)
        volts, amps = own[n_out - 1, h, 0:ports], own[n_out - 1, h, ports:2 * ports]
        a = (volts + zcol * amps) / root
        gath[h, mine, :] = a
        for step in range(1, n_port):
            g_copy(step, h).start()
        power = power + jnp.sum(a * a, axis=1, keepdims=True)

    def p_copy(step):
        return pltpu.make_async_remote_copy(
            src_ref=pbuf.at[0], dst_ref=pbuf.at[step],
            send_sem=p_send.at[step - 1], recv_sem=p_got.at[step - 1],
            device_id={"tm": lax.rem(me + step, n_tm)},
        )

    def m_copy(step):
        return pltpu.make_async_remote_copy(
            src_ref=mbuf.at[port], dst_ref=mbuf.at[port],
            send_sem=m_send.at[step - 1], recv_sem=m_got.at[step - 1],
            device_id={"port": lax.rem(port + step, n_port)},
        )

    diagonal = lane == lax.broadcasted_iota(jnp.int32, (ports, 128), 0)
    packed = jnp.sum(jnp.where(diagonal, power, 0.0), axis=0, keepdims=True)
    pbuf[0] = jnp.broadcast_to(packed, (8, 128))
    for step in range(1, n_tm):
        p_copy(step).start()
    powers = pbuf[0]
    for step in range(1, n_tm):
        p_copy(step).wait_recv()
        powers = powers + pbuf[step]
    mbuf[port] = powers / width + 1e-06
    for step in range(1, n_port):
        m_copy(step).start()
    for step in range(1, n_port):
        m_copy(step).wait_recv()
    for index in range(n_port):
        spread = jnp.broadcast_to(mbuf[index][0:1, :], (ports, 128))
        column = jnp.sum(jnp.where(diagonal, spread, 0.0), axis=1, keepdims=True)
        mcol[index * ports:(index + 1) * ports, :] = jnp.broadcast_to(column, (ports, 128))
    for h in range(subs):
        for step in range(1, n_port):
            g_copy(step, h).wait_recv()
    for p in range(ports):
        q = pair_ref[p]
        for h in range(subs):
            qa[h, p:p + 1, :] = gath[h, pl.ds(q, 1), :]
        qm[p:p + 1, :] = mcol[pl.ds(q, 1), :]
    least = 0.1 * qm[:, 0:1]
    for h in range(subs):
        volts, amps = own[n_out - 1, h, 0:ports], own[n_out - 1, h, ports:2 * ports]
        b = (volts - zcol * amps) / root
        b_re, b_im = b[:, 0:sub], b[:, sub:2 * sub]
        q_re, q_im = qa[h, :, 0:sub], qa[h, :, sub:2 * sub]
        denom = jnp.maximum(q_re * q_re + q_im * q_im, least)
        out_ref[0, :, h * sub:(h + 1) * sub] = (b_re * q_re + b_im * q_im) / denom
        out_ref[1, :, h * sub:(h + 1) * sub] = (b_im * q_re - b_re * q_im) / denom

    for h in range(subs):
        for k in range(n_out):
            for r in range(n_in - 1):
                y_copy(k, r, h).wait_send()
        for k in range(n_out - 1):
            d = destination(k)
            for side in range(2):

                @pl.when(d > outer if side == 0 else d < outer)
                def _():
                    z_copy(k, d, h, side).wait_send()

        for step in range(1, n_port):
            g_copy(step, h).wait_send()
    for step in range(1, n_tm):
        p_copy(step).wait_send()
    for step in range(1, n_port):
        m_copy(step).wait_send()


def body(n_tm, n_port, voltages, currents, impedance, freq_index, window_start, pairing):
    ports, local_times = voltages.shape
    width = freq_index.shape[0]
    total = local_times * n_tm
    assert total & (total - 1) == 0 and ports <= 128
    half = math.gcd(local_times // 2, 1024)
    blocks = local_times // (2 * half)
    groups = half // BASE
    lines = width // n_tm
    n_in = 2 if n_tm < 16 else 4
    n_out = n_tm // n_in
    rows = 2 * ports
    subs = 2 if lines % 256 == 0 else 1
    part = (rows, 2 * (lines // subs))
    tall = BASE + groups + blocks
    assert groups % 8 == 0 and blocks % 8 == 0
    sizes = (n_tm, n_in, n_port, ports, half, blocks, lines, groups, width, subs)
    vmem = pl.BlockSpec(memory_space=pltpu.VMEM)
    dma = pltpu.SemaphoreType.DMA
    return pl.pallas_call(
        functools.partial(kernel, sizes),
        out_shape=jax.ShapeDtypeStruct((2, ports, lines), F32),
        in_specs=[
            pl.BlockSpec(memory_space=pl.ANY), pl.BlockSpec(memory_space=pl.ANY),
            vmem, vmem, vmem, pl.BlockSpec(memory_space=pltpu.SMEM),
        ],
        out_specs=vmem,
        scratch_shapes=[
            pltpu.VMEM((tall, width), F32),
            pltpu.VMEM((tall, width), F32),
            pltpu.VMEM((ports, local_times), F32),
            pltpu.VMEM((ports, local_times), F32),
            pltpu.VMEM((blocks * rows, half), jnp.bfloat16),
            pltpu.VMEM((blocks * rows, half), jnp.bfloat16),
            pltpu.VMEM((half, lines), jnp.bfloat16),
            pltpu.VMEM((half, lines), jnp.bfloat16),
            pltpu.VMEM((n_out, n_in - 1, subs) + part, F32),
            pltpu.VMEM((n_out, subs) + part, F32),
            pltpu.VMEM((n_out, n_in - 1, subs) + part, F32),
            pltpu.VMEM((2, n_out, subs) + part, F32),
            pltpu.VMEM((subs, n_port * ports, part[1]), F32),
            pltpu.VMEM((n_tm, 8, 128), F32),
            pltpu.VMEM((n_port, 8, 128), F32),
            pltpu.VMEM((n_port * ports, 128), F32),
            pltpu.VMEM((subs, ports, part[1]), F32),
            pltpu.VMEM((ports, 128), F32),
            dma((2, blocks)),
            dma((n_out, n_in - 1, subs)), dma((n_out, n_in - 1, subs)),
            dma((n_out, subs)), dma((2, n_out, subs)),
            dma((n_port - 1, subs)), dma((n_port - 1, subs)),
            dma((n_tm - 1,)), dma((n_tm - 1,)),
            dma((n_port - 1,)), dma((n_port - 1,)),
        ],
        compiler_params=pltpu.CompilerParams(
            collective_id=0, has_side_effects=True, vmem_limit_bytes=56 * 2**20
        ),
        name="spectra",
    )(voltages, currents, freq_index[None, :], impedance[None, :], window_start[None, :], pairing)


def solution(mesh):
    placed = (P("port", "tm"), P("port", "tm"), P("port"), P(), P("port"), P("port"))
    return jax.shard_map(
        functools.partial(body, mesh.shape["tm"], mesh.shape["port"]),
        mesh=mesh, in_specs=placed, out_specs=P(None, "port", "tm"), check_vma=False,
    )
```

time: 58.6 us -> 52.8 us (0.901); the launches traced: 57.8 us -> 52.6 us
  other arithmetic: 3.95 us -> 0 us
  local copies, waits for them, and re-layouts: 4.27 us -> 1.57 us
  Pallas kernels: 49.6 us -> 51.1 us
    mul x2 -> x0, other arithmetic: 3.87 us -> none  [the longest x1 3.86 us: body(): sines = jnp.sin(angle) * scale[:, None]]
    broadcast_in_dim x2 -> x0, local copies, waits for them, and re-layouts: 2.7 us -> none  [the longest x1 1.36 us: body(): impedance[:, None]]
    pallas_call x1, Pallas kernels: 49.6 us -> 51.1 us  [body(): pl.pallas_call(functools.partial(kernel, sizes), out_shape=jax.ShapeDtype...]
where the time goes in v2:
time: 52.8 us; the launch traced here: 52.6 us
  Pallas kernels  51.1 us (97%)
  local copies, waits for them, and re-layouts  1.57 us (3%)
    pallas_call x1, Pallas kernels, body(): pl.pallas_call(functools.partial(kernel, sizes), out_shape=jax.ShapeDtype...  51.1 us
    unnamed x1, local copies, waits for them, and re-layouts  1.57 us

profile of v2, /device:TPU:0, one launch (start us, length us, event | category | flops | bytes accessed | tf_op | source)
XLA Modules:
  0.0 52.6 jit_solution(10494044360545228502)
XLA Ops:
  0.0 51.1 %spectra.1 = f32[2,64,256]{2,1,0:T(8,128)} custom-call(f32[64,16384]{1,0:T(8,128)} %v_hbm.1, f32[64,16384]{1,0:T(8,128)} %c_hbm.1, s32[1,2048]{1,0:T(1,128)} %bitcast.3, f32[1,64]{1,0:T(1,128)} %bitcast.4, s32[1,64]{1,0:T(1,128)} %bitcast.5, s32[64]{0:T(128)} %pair_ref.1), custom_call_target="tpu_custom_call" | custom-call | tf_op jit(solution)/shard_map/spectra/pallas_call | solution.py:310
  51.1 1.6 %copy.8 = f32[2,64,256]{2,1,0:T(8,128)} copy(f32[2,64,256]{2,1,0:T(8,128)} %spectra.1) | data formatting | bytes 262144

commit v3 on v2

--- a/solution.py
+++ b/solution.py
@@ -132,12 +132,12 @@
             store[h, :, sub:2 * sub] = im[:, h * sub:(h + 1) * sub]
 
     def destination(k):
-        code, step, place, bit = 0, n_out - 1 - k, outer, 1
-        for _ in range((n_out - 1).bit_length()):
-            one, two = lax.rem(step, 2), lax.rem(place, 2)
-            code = code + bit * (one + two - 2 * one * two)
-            step, place, bit = step // 2, place // 2, 2 * bit
-        return code
+        last = n_out - 1
+        high = outer // (n_out // 2)
+        place = high * outer + (1 - high) * (last - outer)
+        longer = (last + place - k) // n_out
+        row = longer * k + (1 - longer) * (last - k + place)
+        return high * row + (1 - high) * (last - row)
 
     def y_copy(k, r, h):
         return pltpu.make_async_remote_copy(
@@ -188,13 +188,14 @@
                 y_copy(k, r, h).start()
         spectra(target * n_in + inner, own.at[k])
 
-        @pl.when(k >= 1)
+        @pl.when(k >= 2)
         def _():
-            service(k - 1)
+            service(k - 2)
 
         return carry
 
     lax.fori_loop(0, n_out, stage, 0)
+    service(n_out - 2)
 
     mine = pl.ds(pl.multiple_of(port * ports, ports), ports)
 
@@ -244,29 +245,33 @@
     mbuf[port] = powers / width + 1e-06
     for step in range(1, n_port):
         m_copy(step).start()
+    for h in range(subs):
+        for step in range(1, n_port):
+            g_copy(step, h).wait_recv()
+    for h in range(subs):
+        for p in range(ports):
+            qa[h, p:p + 1, :] = gath[h, pl.ds(pair_ref[p], 1), :]
+        volts, amps = own[n_out - 1, h, 0:ports], own[n_out - 1, h, ports:2 * ports]
+        b = (volts - zcol * amps) / root
+        b_re, b_im = b[:, 0:sub], b[:, sub:2 * sub]
+        q_re, q_im = qa[h, :, 0:sub], qa[h, :, sub:2 * sub]
+        out_ref[0, :, h * sub:(h + 1) * sub] = b_re * q_re + b_im * q_im
+        out_ref[1, :, h * sub:(h + 1) * sub] = b_im * q_re - b_re * q_im
     for step in range(1, n_port):
         m_copy(step).wait_recv()
     for index in range(n_port):
         spread = jnp.broadcast_to(mbuf[index][0:1, :], (ports, 128))
         column = jnp.sum(jnp.where(diagonal, spread, 0.0), axis=1, keepdims=True)
         mcol[index * ports:(index + 1) * ports, :] = jnp.broadcast_to(column, (ports, 128))
-    for h in range(subs):
-        for step in range(1, n_port):
-            g_copy(step, h).wait_recv()
     for p in range(ports):
-        q = pair_ref[p]
-        for h in range(subs):
-            qa[h, p:p + 1, :] = gath[h, pl.ds(q, 1), :]
-        qm[p:p + 1, :] = mcol[pl.ds(q, 1), :]
+        qm[p:p + 1, :] = mcol[pl.ds(pair_ref[p], 1), :]
     least = 0.1 * qm[:, 0:1]
     for h in range(subs):
-        volts, amps = own[n_out - 1, h, 0:ports], own[n_out - 1, h, ports:2 * ports]
-        b = (volts - zcol * amps) / root
-        b_re, b_im = b[:, 0:sub], b[:, sub:2 * sub]
         q_re, q_im = qa[h, :, 0:sub], qa[h, :, sub:2 * sub]
         denom = jnp.maximum(q_re * q_re + q_im * q_im, least)
-        out_ref[0, :, h * sub:(h + 1) * sub] = (b_re * q_re + b_im * q_im) / denom
-        out_ref[1, :, h * sub:(h + 1) * sub] = (b_im * q_re - b_re * q_im) / denom
+        for part in range(2):
+            at = (part, slice(None), slice(h * sub, (h + 1) * sub))
+            out_ref[at] = out_ref[at] / denom
 
     for h in range(subs):
         for k in range(n_out):

time: 52.8 us -> 47.7 us (0.903)
  Pallas kernels: 51.1 us -> 45.9 us
    pallas_call x1, Pallas kernels: 51.1 us -> 45.9 us  [body(): pl.pallas_call(functools.partial(kernel, sizes), out_shape=jax.ShapeDtype...]
where the time goes in v3:
time: 47.7 us; the launch traced here: 47.5 us
  Pallas kernels  45.9 us (96%)
  local copies, waits for them, and re-layouts  1.57 us (3%)
    pallas_call x1, Pallas kernels, body(): pl.pallas_call(functools.partial(kernel, sizes), out_shape=jax.ShapeDtype...  45.9 us
    unnamed x1, local copies, waits for them, and re-layouts  1.57 us

profile of v3, /device:TPU:0, one launch (start us, length us, event | category | flops | bytes accessed | tf_op | source)
XLA Modules:
  0.0 47.5 jit_solution(3673245264837102700)
XLA Ops:
  0.0 45.9 %spectra.1 = f32[2,64,256]{2,1,0:T(8,128)} custom-call(f32[64,16384]{1,0:T(8,128)} %v_hbm.1, f32[64,16384]{1,0:T(8,128)} %c_hbm.1, s32[1,2048]{1,0:T(1,128)} %bitcast.3, f32[1,64]{1,0:T(1,128)} %bitcast.4, s32[1,64]{1,0:T(1,128)} %bitcast.5, s32[64]{0:T(128)} %pair_ref.1), custom_call_target="tpu_custom_call" | custom-call | tf_op jit(solution)/shard_map/spectra/pallas_call | solution.py:315
  45.9 1.6 %copy.8 = f32[2,64,256]{2,1,0:T(8,128)} copy(f32[2,64,256]{2,1,0:T(8,128)} %spectra.1) | data formatting | bytes 262144

commit v4 on v3

--- a/solution.py
+++ b/solution.py
@@ -14,10 +14,10 @@
 
 def kernel(
     sizes,
-    v_hbm, c_hbm, freq_ref, z_ref, start_ref, pair_ref,
+    v_hbm, c_hbm, freq_ref, z_ref, start_ref, row_ref, pair_ref,
     out_ref,
     cos_ref, sin_ref,
-    xv, xc, xe, xo, tab_c, tab_s, away, own, y_recv, z_recv, gath, pbuf, mbuf, mcol, qa, qm,
+    xv, xc, xe, xo, tab_c, tab_s, away, own, y_recv, z_recv, gath, pbuf, mbuf, qa,
     load_sem, y_send, y_got, z_send, z_got, g_send, g_got, p_send, p_got, m_send, m_got,
 ):
     n_tm, n_in, n_port, ports, half, blocks, lines, groups, width, subs = sizes
@@ -63,6 +63,7 @@
 
     zcol = column_of(z_ref[...])
     start_column = column_of(start_ref[...].astype(F32)).astype(jnp.int32)
+    pair_column = column_of(row_ref[...].astype(F32)).astype(jnp.int32)
     starts = jnp.broadcast_to(start_column, (ports, 128)) - me * (blocks * span) - lane
 
     whole = n_tm * blocks * span
@@ -259,13 +260,12 @@
         out_ref[1, :, h * sub:(h + 1) * sub] = b_im * q_re - b_re * q_im
     for step in range(1, n_port):
         m_copy(step).wait_recv()
+    chosen = jnp.zeros((ports, 128), F32)
     for index in range(n_port):
         spread = jnp.broadcast_to(mbuf[index][0:1, :], (ports, 128))
-        column = jnp.sum(jnp.where(diagonal, spread, 0.0), axis=1, keepdims=True)
-        mcol[index * ports:(index + 1) * ports, :] = jnp.broadcast_to(column, (ports, 128))
-    for p in range(ports):
-        qm[p:p + 1, :] = mcol[pl.ds(pair_ref[p], 1), :]
-    least = 0.1 * qm[:, 0:1]
+        hit = (lane + index * ports == pair_column) & (lane < ports)
+        chosen = chosen + jnp.where(hit, spread, 0.0)
+    least = 0.1 * jnp.sum(chosen, axis=1, keepdims=True)
     for h in range(subs):
         q_re, q_im = qa[h, :, 0:sub], qa[h, :, sub:2 * sub]
         denom = jnp.maximum(q_re * q_re + q_im * q_im, least)
@@ -317,7 +317,7 @@
         out_shape=jax.ShapeDtypeStruct((2, ports, lines), F32),
         in_specs=[
             pl.BlockSpec(memory_space=pl.ANY), pl.BlockSpec(memory_space=pl.ANY),
-            vmem, vmem, vmem, pl.BlockSpec(memory_space=pltpu.SMEM),
+            vmem, vmem, vmem, vmem, pl.BlockSpec(memory_space=pltpu.SMEM),
         ],
         out_specs=vmem,
         scratch_shapes=[
@@ -336,9 +336,7 @@
             pltpu.VMEM((subs, n_port * ports, part[1]), F32),
             pltpu.VMEM((n_tm, 8, 128), F32),
             pltpu.VMEM((n_port, 8, 128), F32),
-            pltpu.VMEM((n_port * ports, 128), F32),
             pltpu.VMEM((subs, ports, part[1]), F32),
-            pltpu.VMEM((ports, 128), F32),
             dma((2, blocks)),
             dma((n_out, n_in - 1, subs)), dma((n_out, n_in - 1, subs)),
             dma((n_out, subs)), dma((2, n_out, subs)),
@@ -350,7 +348,7 @@
             collective_id=0, has_side_effects=True, vmem_limit_bytes=56 * 2**20
         ),
         name="spectra",
-    )(voltages, currents, freq_index[None, :], impedance[None, :], window_start[None, :], pairing)
+    )(voltages, currents, freq_index[None, :], impedance[None, :], window_start[None, :], pairing[None, :], pairing)
 
 
 def solution(mesh):

time: 47.7 us -> 47.5 us (level)
  no operation moved by 1% of the time
where the time goes in v4:
time: 47.5 us; the launch traced here: 47.3 us
  Pallas kernels  45.8 us (96%)
  local copies, waits for them, and re-layouts  1.57 us (3%)
    pallas_call x1, Pallas kernels, body(): pl.pallas_call(functools.partial(kernel, sizes), out_shape=jax.ShapeDtype...  45.8 us
    unnamed x1, local copies, waits for them, and re-layouts  1.57 us

profile of v4, /device:TPU:0, one launch (start us, length us, event | category | flops | bytes accessed | tf_op | source)
XLA Modules:
  0.0 47.3 jit_solution(5235283864897921869)
XLA Ops:
  0.0 45.8 %spectra.1 = f32[2,64,256]{2,1,0:T(8,128)} custom-call(f32[64,16384]{1,0:T(8,128)} %v_hbm.1, f32[64,16384]{1,0:T(8,128)} %c_hbm.1, s32[1,2048]{1,0:T(1,128)} %bitcast.4, f32[1,64]{1,0:T(1,128)} %bitcast.6, s32[1,64]{1,0:T(1,128)} %bitcast.7, s32[1,64]{1,0:T(1,128)} %bitcast.5, s32[64]{0:T(128)} %pair_ref.1), custom_call_target="tpu_custom_call" | custom-call | tf_op jit(solution)/shard_map/spectra/pallas_call | solution.py:315
  45.8 1.6 %copy.8 = f32[2,64,256]{2,1,0:T(8,128)} copy(f32[2,64,256]{2,1,0:T(8,128)} %spectra.1) | data formatting | bytes 262144
